TPU v7x, 32 devices: a whole 2x2x4 slice. The times are simulated.
32 devices in a mesh: grp: 2 (over y), lab: 4 (over z), dp: 2 (over x), sub: 2 (over core).
Axes of the slice: x: 2, y: 2, z: 4, core: 2. Of those that a mesh axis runs over, the one named last changes fastest.
Arguments:
- enc_rows: bfloat16 [4096, 2048], P(('grp', 'lab', 'dp'), 'sub'), parts along dimension 0, may hold values from -6 to 6
- shortlist: int32 [4096, 8], P(('grp', 'lab', 'dp')), parts along dimension 0, may hold values from 0 to 15, all different within a row; in each aligned block of 256 rows (0 to 255, 256 to 511, ...) at most 256 rows name the same one
- cluster_slot: int32 [16], replicated, may hold values from 0 to 15, each once
- positives: int32 [4096, 16], P(('grp', 'lab', 'dp')), parts along dimension 0, may hold values from 0 to 2047
- panels: bfloat16 [16, 2048, 256], P('lab', 'sub'), may hold values from -0.125 to 0.125
Outputs:
- enc_grad: bfloat16 [4096, 2048], P(('grp', 'lab', 'dp'), 'sub'), parts along dimension 0
- panel_grad: float32 [32, 2048, 256], P(('grp', 'lab', 'dp'), 'sub'), parts along dimension 0
There are 2 independent parts, one for each index of `grp`. A program takes and returns all parts, laid end to end along the dimension named above; an argument that names none is the same for every part. Nothing has to cross between parts.
Inputs may be any that keep to these rules, and one draw needn't show every extreme that they name: `shortlist`: each sample names 8 different clusters. Among the 256 samples of one device (aligned blocks of rows, in order), no cluster is named more than 256 times; in some such blocks a cluster is named exactly 256 times. `cluster_slot`: each panel index occurs once. `positives`: A value v stands for label v % 256 of the sample's shortlisted cluster number v // 256; values may repeat.
All inputs are finite; a program needn't handle non-finite values.
Results may differ from a plain program's by a relative error of at most 0.011.
Values may be sent and summed in bfloat16 or wider, within the bound.
A program may use at most 128 MiB of HBM per device.

v0:
```python
import math

import jax
import jax.numpy as jnp
from jax import lax
from jax.sharding import PartitionSpec as P


def pair_layout(shortlist, cluster_slot, slot_most):
    flat_short = shortlist.reshape(-1)
    cluster_count = cluster_slot.shape[0]
    cluster_ids = jnp.arange(cluster_count, dtype=jnp.int32)
    named = (flat_short[:, None] == cluster_ids[None, :]).astype(jnp.int32)
    panel_slot = jnp.sum(named * cluster_slot[None, :], axis=1)
    placed = (panel_slot[:, None] == cluster_ids[None, :]).astype(jnp.int32)
    ranking = jnp.sum((jnp.cumsum(placed, axis=0) - 1) * placed, axis=1)
    return panel_slot * slot_most + ranking


def body(enc_rows, shortlist, cluster_slot, positives, panels):
    sample_count, half_width = enc_rows.shape
    beam_width = shortlist.shape[1]
    panel_count = panels.shape[0]
    label_width = panels.shape[2]
    lab_count = lax.axis_size("lab")
    cluster_count = panel_count * lab_count
    slot_most = 2 * sample_count * beam_width // cluster_count
    pair_count = sample_count * beam_width
    buffer_size = cluster_count * slot_most
    position = pair_layout(shortlist, cluster_slot, slot_most)
    pair_ids = jnp.arange(pair_count, dtype=jnp.int32)
    filled = jnp.full((buffer_size,), -1, jnp.int32).at[position].set(pair_ids)
    present = filled >= 0
    source = jnp.maximum(filled, 0)
    sent_rows = jnp.where(
        present[:, None],
        jnp.take(enc_rows, source // beam_width, axis=0),
        jnp.zeros((), jnp.bfloat16),
    )
    beam_index = jnp.arange(beam_width, dtype=jnp.int32)
    columns = jnp.where(
        positives[:, None, :] // label_width == beam_index[None, :, None],
        positives[:, None, :] % label_width,
        -1,
    )
    columns = columns.reshape(pair_count, columns.shape[2])
    sent_cols = jnp.where(present[:, None], jnp.take(columns, source, axis=0), -1).astype(
        jnp.bfloat16
    )
    own_count = panels.shape[0]
    send_rows = sent_rows.reshape(lab_count, own_count, slot_most, half_width)
    send_cols = sent_cols.reshape(lab_count, own_count, slot_most, sent_cols.shape[1])
    got_rows, got_cols = (
        lax.all_to_all(send_rows, "lab", split_axis=0, concat_axis=2, tiled=True),
        lax.all_to_all(send_cols, "lab", split_axis=0, concat_axis=2, tiled=True),
    )
    row_total = got_rows.shape[2]
    arrived = got_rows.reshape(own_count, row_total, half_width)
    wanted = got_cols.reshape(own_count, row_total, got_cols.shape[3]).astype(jnp.int32)
    partial_logits = jnp.einsum("crh,chb->crb", arrived, panels, preferred_element_type=jnp.float32)
    logits = lax.psum(partial_logits, "sub")
    block_rows = math.gcd(row_total, 1024)
    block_count = row_total // block_rows
    flat_blocks = own_count * block_count
    label_ids = jnp.arange(label_width, dtype=jnp.int32)

    def block_work(inputs):
        block_index, logit_block, want_block = inputs
        weight = lax.dynamic_index_in_dim(panels, block_index // block_count, 0, keepdims=False)
        target = jnp.any(want_block[:, :, None] == label_ids[None, None, :], axis=1).astype(
            jnp.float32
        )
        grad_block = (jax.nn.sigmoid(logit_block) - target).astype(jnp.bfloat16)
        back_block = jnp.einsum(
            "rb,hb->rh", grad_block, weight, preferred_element_type=jnp.float32
        ).astype(jnp.bfloat16)
        return (back_block, grad_block)

    block_ids = jnp.arange(flat_blocks, dtype=jnp.int32)
    back_rows, logit_grads = lax.map(block_work, (block_ids, logits, wanted))
    back_rows = back_rows.reshape(1, own_count, row_total, half_width)
    returned = lax.all_to_all(back_rows, "lab", split_axis=2, concat_axis=0, tiled=True)
    panel_grad = lax.psum_scatter(
        jnp.einsum("crh,crb->chb", arrived, logit_grads, preferred_element_type=jnp.float32),
        "dp",
        scatter_dimension=0,
        tiled=True,
    )
    returned_flat = returned.reshape(buffer_size, half_width)
    pair_back = jnp.take(returned_flat, position, axis=0).reshape(
        sample_count, beam_width, half_width
    )
    enc_grad = jnp.sum(pair_back, axis=1, dtype=jnp.float32).astype(jnp.bfloat16)
    return (enc_grad, panel_grad)


def solution(mesh):
    in_specs = (
        P(("grp", "lab", "dp"), "sub"),
        P(("grp", "lab", "dp"), None),
        P(),
        P(("grp", "lab", "dp"), None),
        P("lab", "sub", None),
    )
    out_specs = (P(("grp", "lab", "dp"), "sub"), P(("grp", "lab", "dp"), "sub", None))
    return jax.shard_map(body, mesh=mesh, in_specs=in_specs, out_specs=out_specs, check_vma=False)
```

profile of v0, /device:TPU:0, one launch (start us, length us, event | category | flops | bytes accessed | tf_op | source)
XLA Modules:
  0.0 598.4 jit_solution(4624639292844755102)
XLA Ops:
  9.0 4.5 reduce-window.6
  14.4 8.1 %scatter_custom_fusion = s32[4096]{0:T(1024)S(1)} fusion(s32[2048]{0:T(1024)S(1)} %bitcast.96, s32[2048]{0:T(1024)S(1)} %iota.21, s32[]{:T(128)} %constant.148.clone.1), kind=kCustom, calls=%fused_computation.55 | custom fusion | bytes 16388 | tf_op jit(solution)/shard_map/scatter | solution.py:32
  22.5 18.3 %gather_fusion = bf16[4096,1024]{1,0:T(8,128)(2,1)} fusion(bf16[256,1024]{1,0:T(8,128)(2,1)S(1)} %copy-done, s32[4096]{0:T(1024)S(1)} %get-tuple-element.142), kind=kCustom, calls=%fused_computation | custom fusion | bytes 16793600 | tf_op jit(solution)/shard_map/jit(_take)/gather | solution.py:37
  40.8 4.7 select_select_fusion
  45.5 189.2 %all_to_all.39 = bf16[4,4,256,1024]{3,2,1,0:T(8,128)(2,1)} all-to-all(bf16[4,4,256,1024]{3,2,1,0:T(8,128)(2,1)S(1)} %select_select_fusion), channel_id=1, replica_groups=mesh['grp'=2,'lab'=4,'dp'=2,'sub'=2] {'lab'}, dimensions={0} | all-to-all | bytes 16777216 | tf_op jit(solution)/shard_map/all_to_all | solution.py:54
  234.8 8.1 %copy.45 = bf16[1,4,4,256,1024]{4,3,2,1,0:T(8,128)(2,1)} copy(bf16[1,4,4,256,1024]{4,3,1,2,0:T(8,128)(2,1)} %bitcast.88) | data formatting | bytes 16777216 | tf_op jit(solution)/shard_map/all_to_all | solution.py:54
  242.9 7.7 %fusion.18 = f32[4,1024,256]{2,1,0:T(8,128)} fusion(bf16[4,1024,1024]{2,1,0:T(8,128)(2,1)} %bitcast.89, bf16[4,1024,256]{2,1,0:T(8,128)(2,1)S(1)} %copy-done.3), kind=kOutput, calls=%fused_computation.59 | convolution fusion | flops 2147483648 | bytes 14680064 | tf_op jit(solution)/shard_map/crh,chb->crb/dot_general | solution.py:60
  252.0 14.2 %gather_fusion.1 = s32[4096,16]{1,0:T(8,128)} fusion(s32[2048,16]{1,0:T(8,128)S(1)} %bitcast_select_fusion.1, s32[4096]{0:T(1024)S(1)} %get-tuple-element.141), kind=kCustom, calls=%fused_computation.1 | custom fusion | bytes 540672 | tf_op jit(solution)/shard_map/jit(_take)/gather | solution.py:47
  272.4 5.9 all-to-all-done.1
  278.9 80.9 %while.15 = (s32[]{:T(128)}, bf16[4,1024,1024]{2,1,0:T(8,128)(2,1)}, bf16[4,1024,256]{2,1,0:T(8,128)(2,1)}, f32[4,1024,256]{2,1,0:T(8,128)}, s32[4,1024,16]{1,2,...) while((s32[]{:T(128)}, ...), condition=%wide.region_8.9_spmd.clone, body=%wide.region_6.8_spmd.clone.sunk | while | flops 549191680 | bytes 6358683 | solution.py:80
  281.6 11.7 %fusion.29 = pred[1024,256]{1,0:T(8,128)(4,1)S(1)} fusion(s32[1024,16]{1,0:T(8,128)S(1)} %copy.59), kind=kLoop, calls=%fused_computation.6.clone.1 | loop fusion | flops 8126464 | bytes 327680 | tf_op jit(solution)/shard_map/while/body/eval_jaxpr/reduce_or | solution.py:70
  293.3 3.5 bitcast_dynamic-update-slice_fusion.2
  301.9 11.7 %fusion.29 = pred[1024,256]{1,0:T(8,128)(4,1)S(1)} fusion(s32[1024,16]{1,0:T(8,128)S(1)} %copy.59), kind=kLoop, calls=%fused_computation.6.clone.1 | loop fusion | flops 8126464 | bytes 327680 | tf_op jit(solution)/shard_map/while/body/eval_jaxpr/reduce_or | solution.py:70
  322.1 11.7 %fusion.29 = pred[1024,256]{1,0:T(8,128)(4,1)S(1)} fusion(s32[1024,16]{1,0:T(8,128)S(1)} %copy.59), kind=kLoop, calls=%fused_computation.6.clone.1 | loop fusion | flops 8126464 | bytes 327680 | tf_op jit(solution)/shard_map/while/body/eval_jaxpr/reduce_or | solution.py:70
  333.7 3.5 bitcast_dynamic-update-slice_fusion.2
  342.3 11.7 %fusion.29 = pred[1024,256]{1,0:T(8,128)(4,1)S(1)} fusion(s32[1024,16]{1,0:T(8,128)S(1)} %copy.59), kind=kLoop, calls=%fused_computation.6.clone.1 | loop fusion | flops 8126464 | bytes 327680 | tf_op jit(solution)/shard_map/while/body/eval_jaxpr/reduce_or | solution.py:70
  354.0 3.5 bitcast_dynamic-update-slice_fusion.2
  359.8 12.1 %copy.57 = bf16[4,1024,1024]{2,0,1:T(4,128)(2,1)} copy(bf16[4,1024,1024]{2,1,0:T(8,128)(2,1)} %get-tuple-element.106) | data formatting | bytes 16777216 | tf_op jit(solution)/shard_map/while | solution.py:80
  371.9 5.7 all-to-all-start.2
  377.8 8.9 %fusion.19 = f32[4,1024,256]{2,1,0:T(8,128)} fusion(bf16[4,1024,1024]{2,1,0:T(8,128)(2,1)} %bitcast.90, bf16[4,1024,256]{2,1,0:T(8,128)(2,1)} %get-tuple-element.107), kind=kOutput, calls=%fused_computation.60 | convolution fusion | flops 2147483648 | bytes 14680064 | tf_op jit(solution)/shard_map/crh,crb->chb/dot_general | solution.py:84
  386.9 174.5 %all-to-all-done.2 = bf16[1,4,1024,1024]{3,1,0,2:T(4,128)(2,1)} async-done(((bf16[1,4,1024,1024]{3,1,0,2:T(4,128)(2,1)}), bf16[1,4,1024,1024]{3,1,0,2:T(4,128)(2,1)}, u32[]{:S(2)}, u32[]{:S(2)}) %all-to-all-start.2) | async-done | bytes 8388640 | tf_op jit(solution)/shard_map/all_to_all | solution.py:82
  561.4 9.7 %copy.51 = bf16[1,4,4,256,1024]{4,3,1,2,0:T(8,128)(2,1)} copy(bf16[1,4,4,256,1024]{4,1,3,2,0:T(4,128)(2,1)} %bitcast.14) | data formatting | bytes 16777216 | tf_op jit(solution)/shard_map/all_to_all | solution.py:82
  571.1 15.5 %gather_fusion.2 = bf16[2048,1024]{1,0:T(8,128)(2,1)} fusion(bf16[4096,1024]{1,0:T(8,128)(2,1)} %bitcast.85, s32[2048]{0:T(1024)S(1)} %broadcast_clamp_fusion.1), kind=kCustom, calls=%fused_computation.2 | custom fusion | bytes 8396800 | tf_op jit(solution)/shard_map/jit(_take)/gather | solution.py:90
  586.6 4.9 fusion.9
  (65 shorter events, 27.1 us)
Async XLA Ops:
  7.2 15.4 %copy-start = (bf16[256,1024]{1,0:T(8,128)(2,1)S(1)}, bf16[256,1024]{1,0:T(8,128)(2,1)}, u32[]{:S(2)}) copy-start(bf16[256,1024]{1,0:T(8,128)(2,1)} %param.7) | copy-start | bytes 1572868
  7.2 271.7 %all-reduce.2.cloned.1.call-start = ((), (), s32[]{:S(2)}) async-start(), calls=%async_computation.4 | async-start | bytes 8388608 | tf_op jit(solution)/shard_map/psum | solution.py:61
  234.8 8.1 %copy-start.3 = (bf16[4,1024,256]{2,1,0:T(8,128)(2,1)S(1)}, bf16[4,1024,256]{2,1,0:T(8,128)(2,1)}, u32[]{:S(2)}) copy-start(bf16[4,1024,256]{2,1,0:T(8,128)(2,1)} %param.11) | copy-start | bytes 6291460
  250.6 0.7 copy-start.2
  269.1 9.2 %all-to-all-start.1 = ((bf16[4,4,256,16]{2,3,1,0:T(8,128)(2,1)}), bf16[4,4,256,16]{2,3,1,0:T(8,128)(2,1)S(1)}, u32[]{:S(2)}, u32[]{:S(2)}) async-start(bf16[4,4,256,16]{2,3,1,0:T(8,128)(2,1)} %select_convert_fusion), calls=%async_computation.1 | async-start | bytes 262144 | tf_op jit(solution)/shard_map/all_to_all | solution.py:55
  371.9 189.5 %all-to-all-start.2 = ((bf16[1,4,1024,1024]{3,1,0,2:T(4,128)(2,1)}), bf16[1,4,1024,1024]{3,1,0,2:T(4,128)(2,1)}, u32[]{:S(2)}, u32[]{:S(2)}) async-start(bf16[1,4,1024,1024]{3,1,0,2:T(4,128)(2,1)} %bitcast.87), calls=%async_computation.2 | async-start | bytes 16777216 | tf_op jit(solution)/shard_map/all_to_all | solution.py:82
  377.6 214.0 %reduce-scatter.2.cloned.1.call-start = ((), (), s32[]{:S(2)}) async-start(), calls=%async_computation.5 | async-start | bytes 6291456 | tf_op jit(solution)/shard_map/reduce_scatter | solution.py:83
  571.1 20.5 %copy-start.1 = (bf16[256,1024]{1,0:T(8,128)(2,1)S(1)}, bf16[256,1024]{1,0:T(8,128)(2,1)}, u32[]{:S(2)}) copy-start(bf16[256,1024]{1,0:T(8,128)(2,1)} %param.7) | copy-start | bytes 1572868
Sparse Core Ops, SparseCore 0:
  250.7 28.1 all-reduce.1
  386.9 55.6 reduce-scatter.1
where the time goes:
time: 599 us; the launch traced here: 598 us
  blocking collectives  189 us (32%)
  waiting for transfers between devices  181 us (30%)
  local copies, waits for them, and re-layouts  94.2 us (16%)
  other arithmetic  72.5 us (12%)
  matrix products  30.5 us (5%)
  between operations  14.3 us (2%)
  starting transfers between devices  9.3 us (2%)
  loops' own time  7.86 us (1%)
    all_to_all x1, blocking collectives, body(): lax.all_to_all(send_rows, 'lab', split_axis=0, concat_axis=2, tiled=True)  189 us
    all_to_all x1, waiting for transfers between devices, body(): lax.all_to_all(back_rows, 'lab', split_axis=2, concat_axis=0, tiled=True)  174 us
    reduce_or x4, other arithmetic, block_work(): jnp.any(want_block[:, :, None] == label_ids[None, None, :], axis=1)  46.6 us
    gather x1, local copies, waits for them, and re-layouts, body(): jnp.take(enc_rows, source // beam_width, axis=0)  18.3 us
    gather x2, local copies, waits for them, and re-layouts, body(): jnp.take(columns, source, axis=0)  16.4 us
    gather x1, local copies, waits for them, and re-layouts, body(): jnp.take(returned_flat, position, axis=0)  15.5 us
    dot_general x4, matrix products, block_work(): jnp.einsum('rb,hb->rh', grad_block, weight, preferred_element_type=jnp.fl...  13.9 us
    while x1, local copies, waits for them, and re-layouts, body(): back_rows, logit_grads = lax.map(block_work, (block_ids, logits, wanted))  12.1 us
  transfers between devices with their start and end apart: 4, of which 3 were waited for; matrix products, arithmetic and copies ran while one was open for 10% of the time, Pallas kernels for 0%

commit v1 on v0

v1 whole, which is shorter than its diff:
```python
import jax
import jax.numpy as jnp
from jax import lax
from jax.sharding import PartitionSpec as P


def label_slots(shortlist, cluster_slot, positives, label_width):
    clusters = jnp.arange(cluster_slot.shape[0], dtype=jnp.int32)
    named = (shortlist[:, :, None] == clusters).astype(jnp.int32)
    slots = jnp.sum(named * cluster_slot, axis=2)
    beams = jnp.arange(shortlist.shape[1], dtype=jnp.int32)
    picked = (positives[:, :, None] // label_width == beams).astype(jnp.int32)
    pos_slot = jnp.sum(picked * slots[:, None, :], axis=2)
    return slots, pos_slot, positives % label_width


def body(enc_rows, shortlist, cluster_slot, positives, panels):
    samples, half = enc_rows.shape
    own, _, width = panels.shape
    labs = lax.axis_size("lab")
    slots, pos_slot, pos_col = label_slots(shortlist, cluster_slot, positives, width)
    ids = jnp.concatenate([slots, pos_slot * width + pos_col], axis=1)
    all_ids = lax.all_gather(ids, "lab", axis=0, tiled=True)
    all_rows = lax.all_gather(enc_rows, "lab", axis=0, tiled=True)
    beam = shortlist.shape[1]
    first = lax.axis_index("lab") * own
    columns = first * width + jnp.arange(own * width, dtype=jnp.int32)
    present = jnp.any(all_ids[:, :beam, None] == columns[None, None, :] // width, axis=1)
    target = jnp.any(all_ids[:, beam:, None] == columns[None, None, :], axis=1)
    flat = panels.transpose(1, 0, 2).reshape(half, own * width)
    partial = jnp.dot(all_rows, flat, preferred_element_type=jnp.float32)
    logits = lax.psum(partial, "sub")
    grad = jnp.where(present, jax.nn.sigmoid(logits) - target.astype(jnp.float32), 0.0)
    grad = grad.astype(jnp.bfloat16)
    back = lax.dot_general(
        grad, flat, (((1,), (1,)), ((), ())), preferred_element_type=jnp.float32
    ).astype(jnp.bfloat16)
    returned = lax.all_to_all(
        back.reshape(labs, samples, half), "lab", split_axis=0, concat_axis=0, tiled=True
    )
    enc_grad = jnp.sum(returned, axis=0, dtype=jnp.float32).astype(jnp.bfloat16)
    part = jnp.einsum(
        "rh,rcb->chb",
        all_rows,
        grad.reshape(labs * samples, own, width),
        preferred_element_type=jnp.float32,
    )
    panel_grad = lax.psum_scatter(part, "dp", scatter_dimension=0, tiled=True)
    return enc_grad, panel_grad


def solution(mesh):
    in_specs = (
        P(("grp", "lab", "dp"), "sub"),
        P(("grp", "lab", "dp"), None),
        P(),
        P(("grp", "lab", "dp"), None),
        P("lab", "sub", None),
    )
    out_specs = (P(("grp", "lab", "dp"), "sub"), P(("grp", "lab", "dp"), "sub", None))
    return jax.shard_map(body, mesh=mesh, in_specs=in_specs, out_specs=out_specs, check_vma=False)
```

time: 599 us -> 180 us (0.30)
  waiting for transfers between devices: 181 us -> 48 us
  blocking collectives: 189 us -> 61.6 us
  local copies, waits for them, and re-layouts: 94.2 us -> 9.48 us
  other arithmetic: 72.5 us -> 30 us
  matrix products: 30.5 us -> 16.3 us
  starting transfers between devices: 9.3 us -> 0.12 us
  loops' own time: 7.86 us -> 0 us
    all_to_all x2 -> x0, waiting for transfers between devices: 180 us -> none  [the longest x1 174 us: body(): lax.all_to_all(back_rows, 'lab', split_axis=2, concat_axis=0, tiled=True)]
    all_to_all x1, blocking collectives: 189 us -> 48 us  [body(): lax.all_to_all(back.reshape(labs, samples, half), 'lab', split_axis=0, co...]
    gather x4 -> x0, local copies, waits for them, and re-layouts: 50.2 us -> none  [the longest x1 18.3 us: body(): jnp.take(enc_rows, source // beam_width, axis=0)]
    all_gather x0 -> x1, waiting for transfers between devices: none -> 47.3 us  [body(): all_rows = lax.all_gather(enc_rows, 'lab', axis=0, tiled=True)]
    reduce_or x4 -> x2, other arithmetic: 46.6 us -> 24.6 us  [the longest x1 13.7 us: body(): target = jnp.any(all_ids[:, beam:, None] == columns[None, None, :], axis=1)]
    all_to_all x2 -> x0, local copies, waits for them, and re-layouts: 17.8 us -> none  [the longest x1 9.69 us: body(): lax.all_to_all(back_rows, 'lab', split_axis=2, concat_axis=0, tiled=True)]
    dot_general x6 -> x3, matrix products: 30.5 us -> 16.3 us  [the longest x1 6.48 us: body(): jnp.einsum('rh,rcb->chb', all_rows, grad.reshape(labs * samples, own, wid...]
    all_gather x0 -> x1, blocking collectives: none -> 13.6 us  [body(): all_ids = lax.all_gather(ids, 'lab', axis=0, tiled=True)]
  transfers between devices with their start and end apart: 4 -> 3, of which waited for: 3 -> 1; matrix products, arithmetic and copies ran while one was open for 10% -> 19% of each run, Pallas kernels for 0% -> 0%
where the time goes in v1:
time: 180 us; the launch traced here: 179 us
  blocking collectives  61.6 us (34%)
  waiting for transfers between devices  48 us (27%)
  other arithmetic  30 us (17%)
  matrix products  16.3 us (9%)
  between operations  13.9 us (8%)
  local copies, waits for them, and re-layouts  9.48 us (5%)
    all_to_all x1, blocking collectives, body(): lax.all_to_all(back.reshape(labs, samples, half), 'lab', split_axis=0, co...  48 us
    all_gather x1, waiting for transfers between devices, body(): all_rows = lax.all_gather(enc_rows, 'lab', axis=0, tiled=True)  47.3 us
    reduce_or x1, other arithmetic, body(): target = jnp.any(all_ids[:, beam:, None] == columns[None, None, :], axis=1)  13.7 us
    all_gather x1, blocking collectives, body(): all_ids = lax.all_gather(ids, 'lab', axis=0, tiled=True)  13.6 us
    reduce_or x1, other arithmetic, body(): jnp.any(all_ids[:, :beam, None] == columns[None, None, :] // width, axis=1)  10.9 us
    unnamed x10, local copies, waits for them, and re-layouts  6.5 us
    dot_general x1, matrix products, body(): jnp.einsum('rh,rcb->chb', all_rows, grad.reshape(labs * samples, own, wid...  6.48 us
    dot_general x1, matrix products, body(): partial = jnp.dot(all_rows, flat, preferred_element_type=jnp.float32)  5.93 us
  transfers between devices with their start and end apart: 3, of which 1 were waited for; matrix products, arithmetic and copies ran while one was open for 19% of the time, Pallas kernels for 0%

profile of v1, /device:TPU:0, one launch (start us, length us, event | category | flops | bytes accessed | tf_op | source)
XLA Modules:
  0.0 179.4 jit_solution(10416752647868098191)
XLA Ops:
  7.2 0.0 all-gather.2.cloned.1.call-start
  7.2 0.7 all-gather.2.cloned.1.call-update
  7.9 0.0 all-reduce.2.cloned.1.call-start
  7.9 3.0 %copy.23 = bf16[4,1024,256]{1,2,0:T(8,128)(2,1)S(1)} copy(bf16[4,1024,256]{2,1,0:T(8,128)(2,1)} %param.9) | data formatting | bytes 4194304 | tf_op args[4]
  10.9 0.0 copy-start
  11.0 47.3 %all-gather.2.cloned.1.call-done = bf16[1024,1024]{1,0:T(8,128)(2,1)} async-done(((bf16[256,1024]{1,0:T(8,128)(2,1)}), bf16[1024,1024]{1,0:T(8,128)(2,1)}) %all-gather.2.cloned.1.call-update) | async-done | bytes 2097168 | tf_op jit(solution)/shard_map/all_gather | solution.py:24
  58.2 5.9 %fusion.7 = f32[1024,1024]{1,0:T(8,128)} fusion(bf16[1024,1024]{1,0:T(8,128)(2,1)} %all-gather.2.cloned.1.call-done, bf16[1024,1024]{0,1:T(8,128)(2,1)S(1)} %bitcast.15), kind=kOutput, calls=%fused_computation.29 | convolution fusion | flops 2147483648 | bytes 8388608 | tf_op jit(solution)/shard_map/dot_general | solution.py:31
  64.2 0.0 all-reduce.2.cloned.1.call-update
  64.2 0.0 reduce-scatter.2.cloned.1.call-start
  64.3 0.6 copy-done.2
  64.9 0.1 select_reduce_fusion.1
  65.1 13.6 %all_gather.6 = s32[1024,24]{0,1:T(8,128)S(1)} all-gather(s32[256,24]{0,1:T(8,128)S(1)} %pad_add_fusion), channel_id=1, replica_groups=mesh['grp'=2,'lab'=4,'dp'=2,'sub'=2] {'lab'}, dimensions={0}, use_global_device_ids=true | all-gather | bytes 122880 | tf_op jit(solution)/shard_map/all_gather | solution.py:23
  78.7 0.2 copy.24
  78.9 0.2 copy.22
  79.1 10.9 %compare_reduce_fusion.1 = pred[1024,1024]{1,0:T(8,128)(4,1)S(1)} fusion(s32[1024]{0:T(1024)S(1)} %get-tuple-element.8, s32[1024,8]{1,0:T(8,128)S(1)} %copy.22), kind=kLoop, calls=%fused_computation.1 | loop fusion | flops 15728640 | bytes 1085440 | tf_op jit(solution)/shard_map/reduce_or | solution.py:28
  90.0 13.7 %compare_reduce_fusion = pred[1024,1024]{1,0:T(8,128)(4,1)} fusion(s32[1024]{0:T(1024)S(1)} %get-tuple-element.9, s32[1024,16]{1,0:T(8,128)S(1)} %copy.24), kind=kLoop, calls=%fused_computation | loop fusion | flops 32505856 | bytes 1118208 | tf_op jit(solution)/shard_map/reduce_or | solution.py:29
  103.8 3.9 %select_convert_fusion = bf16[1024,1024]{1,0:T(8,128)(2,1)S(1)} fusion(pred[1024,1024]{1,0:T(8,128)(4,1)S(1)} %compare_reduce_fusion.1, pred[1024,1024]{1,0:T(8,128)(4,1)} %compare_reduce_fusion, f32[1024,1024]{1,0:T(8,128)} %all-reduce.2.cloned.1.call-done), kind=kLoop, calls=%fused_computation.2 | loop fusion | flops 7340032 | bytes 8388608 | tf_op jit(solution)/shard_map/convert_element_type | solution.py:34
  107.7 2.6 %copy.27 = bf16[1024,1024]{0,1:T(8,128)(2,1)} copy(bf16[1024,1024]{1,0:T(8,128)(2,1)S(1)} %select_convert_fusion) | data formatting | bytes 4194304 | tf_op jit(solution)/shard_map/reshape | solution.py:45
  110.3 6.5 %convolution_bitcast_fusion = f32[4,1024,256]{1,2,0:T(8,128)} fusion(bf16[1024,4,256]{0,2,1:T(8,128)(2,1)} %bitcast.18, bf16[1024,1024]{1,0:T(8,128)(2,1)} %all-gather.2.cloned.1.call-done), kind=kOutput, calls=%fused_computation.3 | convolution fusion | flops 2147483648 | bytes 8388608 | tf_op jit(solution)/shard_map/rh,rcb->chb/dot_general | solution.py:42
  116.8 0.0 reduce-scatter.2.cloned.1.call-update
  116.8 3.9 %convolution_convert_fusion = bf16[1024,1024]{1,0:T(8,128)(2,1)S(1)} fusion(bf16[1024,1024]{1,0:T(8,128)(2,1)S(1)} %select_convert_fusion, bf16[1024,1024]{0,1:T(8,128)(2,1)} %bitcast.16), kind=kOutput, calls=%fused_computation.5 | convolution fusion | flops 2148532224 | bytes 6291456 | tf_op jit(solution)/shard_map/dot_general | solution.py:35
  120.7 48.0 %all_to_all.5 = bf16[4,256,1024]{2,1,0:T(8,128)(2,1)S(1)} all-to-all(bf16[4,256,1024]{2,1,0:T(8,128)(2,1)S(1)} %bitcast.17), channel_id=1, replica_groups=mesh['grp'=2,'lab'=4,'dp'=2,'sub'=2] {'lab'}, dimensions={0} | all-to-all | bytes 4194304 | tf_op jit(solution)/shard_map/all_to_all | solution.py:38
  168.7 1.3 reduce_sum.32
  170.0 2.9 %copy.26 = f32[2,1024,256]{2,1,0:T(8,128)} copy(f32[2,1024,256]{1,2,0:T(8,128)} %reduce-scatter.2.cloned.1.call-done) | data formatting | bytes 4194304
  (15 shorter events, 0.1 us)
Async XLA Ops:
  7.2 51.1 %all-gather.2.cloned.1.call-start = ((), (), s32[]{:S(2)}) async-start(), calls=%async_computation.2 | async-start | bytes 2621440 | tf_op jit(solution)/shard_map/all_gather | solution.py:24
  7.9 95.9 %all-reduce.2.cloned.1.call-start = ((), (), s32[]{:S(2)}) async-start(), calls=%async_computation.3 | async-start | bytes 8388608 | tf_op jit(solution)/shard_map/psum | solution.py:32
  10.9 53.2 %copy-start = (bf16[4,1024,256]{1,2,0:T(8,128)(2,1)}, bf16[4,1024,256]{1,2,0:T(8,128)(2,1)S(1)}, u32[]{:S(2)}) copy-start(bf16[4,1024,256]{1,2,0:T(8,128)(2,1)S(1)} %copy.23) | copy-start | bytes 6291460
  64.2 0.7 copy-start.2
  64.2 0.7 copy-start.3
  64.2 0.8 copy-start.1
  64.2 105.8 %reduce-scatter.2.cloned.1.call-start = ((), (), s32[]{:S(2)}) async-start(), calls=%async_computation.4 | async-start | bytes 6291456 | tf_op jit(solution)/shard_map/reduce_scatter | solution.py:48
Sparse Core Ops, SparseCore 0:
  9.6 48.6 all-gather.1
  64.3 27.1 all-reduce.1
  116.9 52.8 reduce-scatter.1

commit v2 on v1

--- a/solution.py
+++ b/solution.py
@@ -1,6 +1,10 @@
+import functools
+
 import jax
 import jax.numpy as jnp
 from jax import lax
+from jax.experimental import pallas as pl
+from jax.experimental.pallas import tpu as pltpu
 from jax.sharding import PartitionSpec as P
 
 
@@ -14,7 +18,7 @@
     return slots, pos_slot, positives % label_width
 
 
-def body(enc_rows, shortlist, cluster_slot, positives, panels):
+def array_body(enc_rows, shortlist, cluster_slot, positives, panels):
     samples, half = enc_rows.shape
     own, _, width = panels.shape
     labs = lax.axis_size("lab")
@@ -49,6 +53,315 @@
     return enc_grad, panel_grad
 
 
+CUTS = 2
+MESH = pl.DeviceIdType.MESH
+
+
+def unit_of(u, me, labs):
+    pairs = jnp.minimum(me, labs - 1 - me)
+    longer = jnp.where(2 * me < labs - 1, 1, -1)
+    v = u - CUTS
+    w = v % (2 * CUTS)
+    near = me + (v // (2 * CUTS) + 1) * (2 * (w % 2) - 1)
+    x = v - 2 * CUTS * pairs
+    far = me + longer * (pairs + 1 + x // CUTS)
+    block = jnp.where(u < CUTS, me, jnp.where(x < 0, near, far))
+    cut = jnp.where(u < CUTS, u, jnp.where(x < 0, w // 2, x % CUTS))
+    return block, cut
+
+
+def step_kernel(
+    dims, enc_ref, ids_ref, panel_ref, enc_out, panel_out,
+    rows, rows_t, ids_buf, part, other, want, grads, held, sent, got, share_out, share_in,
+    row_send, row_recv, id_send, id_recv, lx_send, lx_recv, rt_send, rt_recv, sh_send, sh_recv,
+):
+    labs, dps, own, beam, picks, width = dims
+    size = enc_ref.shape[1]
+    half = enc_ref.shape[2]
+    me = lax.axis_index("lab")
+    dp = lax.axis_index("dp")
+    core = lax.axis_index("sub")
+    left, right = jnp.maximum(me - 1, 0), jnp.minimum(me + 1, labs - 1)
+    keep = own // dps
+
+    barrier = pltpu.get_barrier_semaphore()
+    for off in range(1, labs):
+        pl.semaphore_signal(barrier, inc=1, device_id={"lab": (me + off) % labs}, device_id_type=MESH)
+    for off in range(1, dps):
+        pl.semaphore_signal(barrier, inc=1, device_id={"dp": (dp + off) % dps}, device_id_type=MESH)
+    pl.semaphore_signal(barrier, inc=1, device_id={"sub": 1 - core}, device_id_type=MESH)
+    pl.semaphore_wait(barrier, labs + dps - 1)
+
+    def remote(src, dst, send, recv, where):
+        return pltpu.make_async_remote_copy(
+            src_ref=src, dst_ref=dst, send_sem=send, recv_sem=recv,
+            device_id=where, device_id_type=MESH,
+        )
+
+    def row_copy(src, block, cut, side):
+        return remote(
+            src, rows.at[block, cut], row_send.at[side, block, cut], row_recv.at[block, cut],
+            {"lab": left if side == 0 else right},
+        )
+
+    def id_copy(off):
+        return remote(
+            ids_ref, ids_buf.at[me], id_send.at[off], id_recv.at[me], {"lab": (me + off) % labs}
+        )
+
+    def id_arrival(block):
+        return remote(ids_ref, ids_buf.at[block], id_send.at[0], id_recv.at[block], {"lab": left})
+
+    def lx_copy(block, cut):
+        return remote(
+            part.at[block, cut], other.at[block, cut],
+            lx_send.at[block, cut], lx_recv.at[block, cut], {"sub": 1 - core},
+        )
+
+    def back_copy(block, cut, side):
+        return remote(
+            sent.at[block, cut], got.at[side, block, cut],
+            rt_send.at[block, cut], rt_recv.at[side, block, cut],
+            {"lab": right if side == 0 else left},
+        )
+
+    def share_copy(off, j):
+        return remote(
+            share_out.at[off - 1, j], share_in.at[off - 1, j],
+            sh_send.at[off - 1, j], sh_recv.at[off - 1, j], {"dp": (dp + off) % dps},
+        )
+
+    for off in range(1, labs):
+        id_copy(off).start()
+    for cut in range(CUTS):
+        @pl.when(me > 0)
+        def _():
+            row_copy(enc_ref.at[cut], me, cut, 0).start()
+
+        @pl.when(me < labs - 1)
+        def _():
+            row_copy(enc_ref.at[cut], me, cut, 1).start()
+
+    rows[me] = enc_ref[...]
+    ids_buf[me] = ids_ref[...]
+    lane = lax.broadcasted_iota(jnp.int32, (1, width), 1).astype(jnp.float32)
+
+    @pl.loop(0, labs * CUTS)
+    def _(u):
+        block, cut = unit_of(u, me, labs)
+
+        @pl.when(block != me)
+        def _():
+            row_copy(enc_ref.at[0], block, cut, 0).wait_recv()
+
+        @pl.when((block < me) & (me < labs - 1))
+        def _():
+            row_copy(rows.at[block, cut], block, cut, 1).start()
+
+        @pl.when((block > me) & (me > 0))
+        def _():
+            row_copy(rows.at[block, cut], block, cut, 0).start()
+
+        unit = rows[block, cut]
+        for c in range(own):
+            part[block, cut, :, c * width:(c + 1) * width] = jnp.dot(
+                unit, panel_ref[c], preferred_element_type=jnp.float32
+            )
+        lx_copy(block, cut).start()
+        rows_t[block, cut] = unit.T
+
+        @pl.when((block != me) & (cut == 0))
+        def _():
+            id_arrival(block).wait_recv()
+
+        ids = ids_buf[block, cut]
+        ids = jnp.concatenate([ids, jnp.zeros((128 - ids.shape[0], size), jnp.float32)], axis=0).T
+        for c in range(own):
+            slot = (me * own + c).astype(jnp.float32)
+            present = jnp.zeros((size, 1), jnp.bool_)
+            for k in range(beam):
+                present = present | (ids[:, k:k + 1] == slot)
+            here = lane + slot * width
+            target = jnp.zeros((size, width), jnp.float32)
+            for i in range(beam, beam + picks):
+                target = jnp.where(ids[:, i:i + 1] == here, 1.0, target)
+            want[:, c * width:(c + 1) * width] = jnp.where(present, target, 2.0)
+
+        lx_copy(block, cut).wait_recv()
+        total = jnp.zeros((size, half), jnp.float32)
+        for c in range(own):
+            cols = slice(c * width, (c + 1) * width)
+            logit = part[block, cut, :, cols] + other[block, cut, :, cols]
+            goal = want[:, cols]
+            grad = jnp.where(goal > 1.5, 0.0, jax.nn.sigmoid(logit) - goal).astype(jnp.bfloat16)
+            grads[block, cut, :, cols] = grad
+            total += lax.dot_general(
+                grad, panel_ref[c], (((1,), (1,)), ((), ())), preferred_element_type=jnp.float32
+            )
+        held[block, cut] = total
+
+        @pl.when((me == 0) & (block > 0))
+        def _():
+            sent[block, cut] = total.astype(jnp.bfloat16)
+            back_copy(block, cut, 0).start()
+
+        @pl.when((me == labs - 1) & (block < me))
+        def _():
+            sent[block, cut] = total.astype(jnp.bfloat16)
+            back_copy(block, cut, 1).start()
+
+    units = [(b, q) for b in range(labs) for q in range(CUTS)]
+
+    def panel_sum(c):
+        wide = jnp.concatenate([rows_t[b, q] for b, q in units], axis=1)
+        tall = jnp.concatenate(
+            [grads[b, q, :, pl.ds(pl.multiple_of(c * width, width), width)] for b, q in units],
+            axis=0,
+        )
+        return jnp.dot(wide, tall, preferred_element_type=jnp.float32)
+
+    for off in range(1, dps):
+        for j in range(keep):
+            share_out[off - 1, j] = panel_sum(((dp + off) % dps) * keep + j).astype(jnp.bfloat16)
+            share_copy(off, j).start()
+    for j in range(keep):
+        panel_out[j] = panel_sum(dp * keep + j)
+
+    def pass_on(block, cut, side):
+        back_copy(block, cut, side).wait_recv()
+        sent[block, cut] = (
+            held[block, cut] + got[side, block, cut].astype(jnp.float32)
+        ).astype(jnp.bfloat16)
+        back_copy(block, cut, side).start()
+
+    for k in range(1, labs):
+        for cut in range(CUTS):
+            @pl.when((me > 0) & (me < k))
+            def _():
+                pass_on(k, cut, 0)
+
+            @pl.when((me > labs - 1 - k) & (me < labs - 1))
+            def _():
+                pass_on(labs - 1 - k, cut, 1)
+
+    for cut in range(CUTS):
+        @pl.when(me > 0)
+        def _():
+            back_copy(me, cut, 0).wait_recv()
+            held[me, cut] += got[0, me, cut].astype(jnp.float32)
+
+        @pl.when(me < labs - 1)
+        def _():
+            back_copy(me, cut, 1).wait_recv()
+            held[me, cut] += got[1, me, cut].astype(jnp.float32)
+
+        enc_out[cut] = held[me, cut].astype(jnp.bfloat16)
+
+    for off in range(1, dps):
+        for j in range(keep):
+            share_copy(off, j).wait_recv()
+            panel_out[j] += share_in[off - 1, j].astype(jnp.float32)
+
+    for off in range(1, labs):
+        id_copy(off).wait_send()
+    for off in range(1, dps):
+        for j in range(keep):
+            share_copy(off, j).wait_send()
+    for block, cut in units:
+        lx_copy(block, cut).wait_send()
+
+        @pl.when((block <= me) & (me < labs - 1))
+        def _():
+            row_copy(enc_ref.at[0], block, cut, 1).wait_send()
+
+        @pl.when((block >= me) & (me > 0))
+        def _():
+            row_copy(enc_ref.at[0], block, cut, 0).wait_send()
+
+        @pl.when(block != me)
+        def _():
+            back_copy(block, cut, 0).wait_send()
+
+
+def kernel_body(enc_rows, shortlist, cluster_slot, positives, panels):
+    samples, half = enc_rows.shape
+    own, _, width = panels.shape
+    labs, dps = lax.axis_size("lab"), lax.axis_size("dp")
+    beam, picks = shortlist.shape[1], positives.shape[1]
+    size = samples // CUTS
+    keep = own // dps
+    slots, pos_slot, pos_col = label_slots(shortlist, cluster_slot, positives, width)
+    ids = jnp.concatenate([slots, pos_slot * width + pos_col], axis=1).astype(jnp.float32)
+    id_rows = -(-(beam + picks) // 8) * 8
+    ids = jnp.pad(ids, ((0, 0), (0, id_rows - beam - picks)), constant_values=-1.0)
+    ids = ids.reshape(CUTS, size, id_rows).transpose(0, 2, 1)
+    f32, bf16 = jnp.float32, jnp.bfloat16
+    vmem, dma = pltpu.VMEM, pltpu.SemaphoreType.DMA
+    whole = pl.BlockSpec(memory_space=pltpu.VMEM)
+    enc_grad, panel_grad = pl.pallas_call(
+        functools.partial(step_kernel, (labs, dps, own, beam, picks, width)),
+        out_shape=(
+            jax.ShapeDtypeStruct((CUTS, size, half), bf16),
+            jax.ShapeDtypeStruct((keep, half, width), f32),
+        ),
+        in_specs=[whole] * 3,
+        out_specs=(whole, whole),
+        scratch_shapes=[
+            vmem((labs, CUTS, size, half), bf16),
+            vmem((labs, CUTS, half, size), bf16),
+            vmem((labs, CUTS, id_rows, size), f32),
+            vmem((labs, CUTS, size, own * width), f32),
+            vmem((labs, CUTS, size, own * width), f32),
+            vmem((size, own * width), f32),
+            vmem((labs, CUTS, size, own * width), bf16),
+            vmem((labs, CUTS, size, half), f32),
+            vmem((labs, CUTS, size, half), bf16),
+            vmem((2, labs, CUTS, size, half), bf16),
+            vmem((dps - 1, keep, half, width), bf16),
+            vmem((dps - 1, keep, half, width), bf16),
+            dma((2, labs, CUTS)),
+            dma((labs, CUTS)),
+            dma((labs,)),
+            dma((labs,)),
+            dma((labs, CUTS)),
+            dma((labs, CUTS)),
+            dma((labs, CUTS)),
+            dma((2, labs, CUTS)),
+            dma((dps - 1, keep)),
+            dma((dps - 1, keep)),
+        ],
+        compiler_params=pltpu.CompilerParams(
+            collective_id=0, has_side_effects=True, vmem_limit_bytes=58 << 20
+        ),
+    )(enc_rows.reshape(CUTS, size, half), ids, panels)
+    return enc_grad.reshape(samples, half), panel_grad
+
+
+def kernel_fits(enc_rows, shortlist, positives, panels):
+    samples, half = enc_rows.shape
+    own, _, width = panels.shape
+    labs, dps = lax.axis_size("lab"), lax.axis_size("dp")
+    unit = labs * samples
+    room = unit * half * 14 + unit * own * width * 10 + 14 * own * half * width
+    return (
+        room < 54 << 20
+        and labs > 1
+        and dps > 1
+        and lax.axis_size("sub") == 2
+        and own % dps == 0
+        and samples % (CUTS * 128) == 0
+        and half % 128 == 0
+        and width % 128 == 0
+        and shortlist.shape[1] + positives.shape[1] <= 128
+    )
+
+
+def body(enc_rows, shortlist, cluster_slot, positives, panels):
+    if kernel_fits(enc_rows, shortlist, positives, panels):
+        return kernel_body(enc_rows, shortlist, cluster_slot, positives, panels)
+    return array_body(enc_rows, shortlist, cluster_slot, positives, panels)
+
+
 def solution(mesh):
     in_specs = (
         P(("grp", "lab", "dp"), "sub"),

time: 180 us -> 96.7 us (0.54)
  Pallas kernels: 0 us -> 87.8 us
  blocking collectives: 61.6 us -> 0 us
  waiting for transfers between devices: 48 us -> 0 us
  other arithmetic: 30 us -> 2.93 us
  matrix products: 16.3 us -> 0 us
  between operations: 13.9 us -> 0.65 us
  local copies, waits for them, and re-layouts: 9.48 us -> 4.91 us
    pallas_call x0 -> x1, Pallas kernels: none -> 87.8 us  [kernel_body(): pl.pallas_call(functools.partial(step_kernel, (labs, dps, own, beam, pick...]
    all_to_all x1 -> x0, blocking collectives: 48 us -> none  [body(): lax.all_to_all(back.reshape(labs, samples, half), 'lab', split_axis=0, co...]
    all_gather x1 -> x0, waiting for transfers between devices: 47.3 us -> none  [body(): all_rows = lax.all_gather(enc_rows, 'lab', axis=0, tiled=True)]
    reduce_or x2 -> x0, other arithmetic: 24.6 us -> none  [the longest x1 13.7 us: body(): target = jnp.any(all_ids[:, beam:, None] == columns[None, None, :], axis=1)]
    dot_general x3 -> x0, matrix products: 16.3 us -> none  [the longest x1 6.48 us: body(): jnp.einsum('rh,rcb->chb', all_rows, grad.reshape(labs * samples, own, wid...]
    all_gather x1 -> x0, blocking collectives: 13.6 us -> none  [body(): all_ids = lax.all_gather(ids, 'lab', axis=0, tiled=True)]
    convert_element_type x1 -> x0, other arithmetic: 3.94 us -> none  [body(): grad = grad.astype(jnp.bfloat16)]
    reshape x1 -> x0, local copies, waits for them, and re-layouts: 2.58 us -> none  [body(): grad.reshape(labs * samples, own, width)]
  transfers between devices with their start and end apart: 3 -> 0, of which waited for: 1 -> 0; matrix products, arithmetic and copies ran while one was open for 19% -> 0% of each run, Pallas kernels for 0% -> 0%
where the time goes in v2:
time: 96.7 us; the launch traced here: 96.3 us
  Pallas kernels  87.8 us (91%)
  local copies, waits for them, and re-layouts  4.91 us (5%)
  other arithmetic  2.93 us (3%)
    pallas_call x1, Pallas kernels, kernel_body(): pl.pallas_call(functools.partial(step_kernel, (labs, dps, own, beam, pick...  87.8 us
    unnamed x2, local copies, waits for them, and re-layouts  4.91 us

profile of v2, /device:TPU:0, one launch (start us, length us, event | category | flops | bytes accessed | tf_op | source)
XLA Modules:
  0.0 96.3 jit_solution(8003377124736450068)
XLA Ops:
  0.6 0.8 select_reduce_fusion.1
  1.4 0.7 add_select_fusion.1
  2.2 0.7 copy_bitcast_fusion
  3.0 0.6 fusion.ids_ref
  3.6 87.8 %shard_map.68 = (bf16[2,128,1024]{2,1,0:T(8,128)(2,1)}, f32[2,1024,256]{2,1,0:T(8,128)}) custom-call(bf16[2,128,1024]{2,1,0:T(8,128)(2,1)} %bitcast.10, f32[2,24,128]{2,1,0:T(8,128)} %fusion.ids_ref, bf16[4,1024,256]{2,1,0:T(8,128)(2,1)} %panel_ref.1), custom_call_target="tpu_custom_call" | custom-call | tf_op jit(solution)/shard_map/pallas_call | solution.py:301
  91.4 1.9 %copy.18 = bf16[256,1024]{1,0:T(8,128)(2,1)} copy(bf16[256,1024]{1,0:T(8,128)(2,1)} %bitcast.11) | data formatting | bytes 1048576
  93.3 3.0 %copy.19 = f32[2,1024,256]{2,1,0:T(8,128)} copy(f32[2,1024,256]{2,1,0:T(8,128)} %get-tuple-element.9) | data formatting | bytes 4194304
  (1 shorter events, 0.0 us)

commit v3 on v2

--- a/solution.py
+++ b/solution.py
@@ -58,15 +58,17 @@
 
 
 def unit_of(u, me, labs):
-    pairs = jnp.minimum(me, labs - 1 - me)
-    longer = jnp.where(2 * me < labs - 1, 1, -1)
-    v = u - CUTS
-    w = v % (2 * CUTS)
-    near = me + (v // (2 * CUTS) + 1) * (2 * (w % 2) - 1)
-    x = v - 2 * CUTS * pairs
-    far = me + longer * (pairs + 1 + x // CUTS)
-    block = jnp.where(u < CUTS, me, jnp.where(x < 0, near, far))
-    cut = jnp.where(u < CUTS, u, jnp.where(x < 0, w // 2, x % CUTS))
+    lefts, rights = me, labs - 1 - me
+    p = u - CUTS
+    both = 2 * jnp.minimum(lefts, rights)
+    paired = p < 2 * both
+    side = jnp.where(paired, p % 2, jnp.where(rights > lefts, 1, 0))
+    s = jnp.where(paired, p // 2, p - both)
+    count = jnp.where(side == 1, rights, lefts)
+    near = s < count
+    far_off = jnp.where(near, s + 1, 2 * count - s)
+    block = jnp.where(u < CUTS, me, me + (2 * side - 1) * far_off)
+    cut = jnp.where(u < CUTS, u, jnp.where(near, 0, 1))
     return block, cut
 
 
@@ -83,6 +85,8 @@
     core = lax.axis_index("sub")
     left, right = jnp.maximum(me - 1, 0), jnp.minimum(me + 1, labs - 1)
     keep = own // dps
+    last_right, cut_right = left, jnp.where(me == 0, 0, 1)
+    last_left, cut_left = right, jnp.where(me == labs - 1, 0, 1)
 
     barrier = pltpu.get_barrier_semaphore()
     for off in range(1, labs):
@@ -133,14 +137,13 @@
 
     for off in range(1, labs):
         id_copy(off).start()
-    for cut in range(CUTS):
-        @pl.when(me > 0)
-        def _():
-            row_copy(enc_ref.at[cut], me, cut, 0).start()
-
-        @pl.when(me < labs - 1)
-        def _():
-            row_copy(enc_ref.at[cut], me, cut, 1).start()
+    @pl.when(me > 0)
+    def _():
+        row_copy(enc_ref.at[0], me, 0, 0).start()
+
+    @pl.when(me < labs - 1)
+    def _():
+        row_copy(enc_ref.at[0], me, 0, 1).start()
 
     rows[me] = enc_ref[...]
     ids_buf[me] = ids_ref[...]
@@ -210,6 +213,16 @@
             sent[block, cut] = total.astype(jnp.bfloat16)
             back_copy(block, cut, 1).start()
 
+        @pl.when((me < labs - 1) & (block == last_right) & (cut == cut_right))
+        def _():
+            row_copy(enc_ref.at[0], block, cut, 1).wait_send()
+            row_copy(enc_ref.at[1], me, 1, 1).start()
+
+        @pl.when((me > 0) & (block == last_left) & (cut == cut_left))
+        def _():
+            row_copy(enc_ref.at[0], block, cut, 0).wait_send()
+            row_copy(enc_ref.at[1], me, 1, 0).start()
+
     units = [(b, q) for b in range(labs) for q in range(CUTS)]
 
     def panel_sum(c):
@@ -219,13 +232,6 @@
             axis=0,
         )
         return jnp.dot(wide, tall, preferred_element_type=jnp.float32)
-
-    for off in range(1, dps):
-        for j in range(keep):
-            share_out[off - 1, j] = panel_sum(((dp + off) % dps) * keep + j).astype(jnp.bfloat16)
-            share_copy(off, j).start()
-    for j in range(keep):
-        panel_out[j] = panel_sum(dp * keep + j)
 
     def pass_on(block, cut, side):
         back_copy(block, cut, side).wait_recv()
@@ -234,15 +240,25 @@
         ).astype(jnp.bfloat16)
         back_copy(block, cut, side).start()
 
+    def pass_all(k, cut):
+        @pl.when((me > 0) & (me < k))
+        def _():
+            pass_on(k, cut, 0)
+
+        @pl.when((me > labs - 1 - k) & (me < labs - 1))
+        def _():
+            pass_on(labs - 1 - k, cut, 1)
+
     for k in range(1, labs):
-        for cut in range(CUTS):
-            @pl.when((me > 0) & (me < k))
-            def _():
-                pass_on(k, cut, 0)
-
-            @pl.when((me > labs - 1 - k) & (me < labs - 1))
-            def _():
-                pass_on(labs - 1 - k, cut, 1)
+        pass_all(k, 0)
+    for off in range(1, dps):
+        for j in range(keep):
+            share_out[off - 1, j] = panel_sum(((dp + off) % dps) * keep + j).astype(jnp.bfloat16)
+            share_copy(off, j).start()
+    for k in range(labs - 1, 0, -1):
+        pass_all(k, 1)
+    for j in range(keep):
+        panel_out[j] = panel_sum(dp * keep + j)
 
     for cut in range(CUTS):
         @pl.when(me > 0)
@@ -270,11 +286,11 @@
     for block, cut in units:
         lx_copy(block, cut).wait_send()
 
-        @pl.when((block <= me) & (me < labs - 1))
+        @pl.when((block <= me) & (me < labs - 1) & ((block != last_right) | (cut != cut_right)))
         def _():
             row_copy(enc_ref.at[0], block, cut, 1).wait_send()
 
-        @pl.when((block >= me) & (me > 0))
+        @pl.when((block >= me) & (me > 0) & ((block != last_left) | (cut != cut_left)))
         def _():
             row_copy(enc_ref.at[0], block, cut, 0).wait_send()
 

time: 96.7 us -> 95.4 us (0.987)
  Pallas kernels: 87.8 us -> 85.7 us
    pallas_call x1, Pallas kernels: 87.8 us -> 85.7 us  [kernel_body(): pl.pallas_call(functools.partial(step_kernel, (labs, dps, own, beam, pick...]
where the time goes in v3:
time: 95.4 us; the launch traced here: 94.2 us
  Pallas kernels  85.7 us (90%)
  local copies, waits for them, and re-layouts  4.91 us (5%)
  other arithmetic  2.93 us (3%)
    pallas_call x1, Pallas kernels, kernel_body(): pl.pallas_call(functools.partial(step_kernel, (labs, dps, own, beam, pick...  85.7 us
    unnamed x2, local copies, waits for them, and re-layouts  4.91 us

profile of v3, /device:TPU:0, one launch (start us, length us, event | category | flops | bytes accessed | tf_op | source)
XLA Modules:
  0.0 94.2 jit_solution(16310636978470921717)
XLA Ops:
  0.6 0.8 select_reduce_fusion.1
  1.4 0.7 add_select_fusion.1
  2.2 0.7 copy_bitcast_fusion
  3.0 0.6 fusion.ids_ref
  3.6 85.7 %shard_map.68 = (bf16[2,128,1024]{2,1,0:T(8,128)(2,1)}, f32[2,1024,256]{2,1,0:T(8,128)}) custom-call(bf16[2,128,1024]{2,1,0:T(8,128)(2,1)} %bitcast.10, f32[2,24,128]{2,1,0:T(8,128)} %fusion.ids_ref, bf16[4,1024,256]{2,1,0:T(8,128)(2,1)} %panel_ref.1), custom_call_target="tpu_custom_call" | custom-call | tf_op jit(solution)/shard_map/pallas_call | solution.py:317
  89.3 1.9 %copy.18 = bf16[256,1024]{1,0:T(8,128)(2,1)} copy(bf16[256,1024]{1,0:T(8,128)(2,1)} %bitcast.11) | data formatting | bytes 1048576
  91.2 3.0 %copy.19 = f32[2,1024,256]{2,1,0:T(8,128)} copy(f32[2,1024,256]{2,1,0:T(8,128)} %get-tuple-element.9) | data formatting | bytes 4194304
  (1 shorter events, 0.0 us)

commit v4 on v3

--- a/solution.py
+++ b/solution.py
@@ -87,6 +87,10 @@
     keep = own // dps
     last_right, cut_right = left, jnp.where(me == 0, 0, 1)
     last_left, cut_left = right, jnp.where(me == labs - 1, 0, 1)
+    lefts, rights = me, labs - 1 - me
+    near_left = lefts <= rights
+    right_turn = jnp.where(me == 0, 0, jnp.where(near_left, CUTS + 4 * lefts - 1, -1))
+    left_turn = jnp.where(rights == 0, 0, jnp.where(near_left, -1, CUTS + 4 * rights))
 
     barrier = pltpu.get_barrier_semaphore()
     for off in range(1, labs):
@@ -134,6 +138,11 @@
             share_out.at[off - 1, j], share_in.at[off - 1, j],
             sh_send.at[off - 1, j], sh_recv.at[off - 1, j], {"dp": (dp + off) % dps},
         )
+
+    def late_half(side):
+        block, cut = (last_left, cut_left) if side == 0 else (last_right, cut_right)
+        row_copy(enc_ref.at[0], block, cut, side).wait_send()
+        row_copy(enc_ref.at[1], me, 1, side).start()
 
     for off in range(1, labs):
         id_copy(off).start()
@@ -213,15 +222,13 @@
             sent[block, cut] = total.astype(jnp.bfloat16)
             back_copy(block, cut, 1).start()
 
-        @pl.when((me < labs - 1) & (block == last_right) & (cut == cut_right))
-        def _():
-            row_copy(enc_ref.at[0], block, cut, 1).wait_send()
-            row_copy(enc_ref.at[1], me, 1, 1).start()
-
-        @pl.when((me > 0) & (block == last_left) & (cut == cut_left))
-        def _():
-            row_copy(enc_ref.at[0], block, cut, 0).wait_send()
-            row_copy(enc_ref.at[1], me, 1, 0).start()
+        @pl.when((me < labs - 1) & (u == right_turn))
+        def _():
+            late_half(1)
+
+        @pl.when((me > 0) & (u == left_turn))
+        def _():
+            late_half(0)
 
     units = [(b, q) for b in range(labs) for q in range(CUTS)]
 
@@ -240,23 +247,47 @@
         ).astype(jnp.bfloat16)
         back_copy(block, cut, side).start()
 
-    def pass_all(k, cut):
+    def pass_right(k, cut):
         @pl.when((me > 0) & (me < k))
         def _():
             pass_on(k, cut, 0)
 
+    def pass_left(k, cut):
         @pl.when((me > labs - 1 - k) & (me < labs - 1))
         def _():
             pass_on(labs - 1 - k, cut, 1)
 
-    for k in range(1, labs):
-        pass_all(k, 0)
+    @pl.when(near_left)
+    def _():
+        for k in range(1, labs):
+            pass_right(k, 0)
+
+        @pl.when(me > 0)
+        def _():
+            late_half(0)
+
+        for k in range(1, labs):
+            pass_left(k, 0)
+
+    @pl.when(jnp.logical_not(near_left))
+    def _():
+        for k in range(1, labs):
+            pass_left(k, 0)
+
+        @pl.when(me < labs - 1)
+        def _():
+            late_half(1)
+
+        for k in range(1, labs):
+            pass_right(k, 0)
+
     for off in range(1, dps):
         for j in range(keep):
             share_out[off - 1, j] = panel_sum(((dp + off) % dps) * keep + j).astype(jnp.bfloat16)
             share_copy(off, j).start()
     for k in range(labs - 1, 0, -1):
-        pass_all(k, 1)
+        pass_right(k, 1)
+        pass_left(k, 1)
     for j in range(keep):
         panel_out[j] = panel_sum(dp * keep + j)
 

time: 95.4 us -> 93.8 us (0.983)
  no operation moved by 1% of the time
where the time goes in v4:
time: 93.8 us; the launch traced here: 93.3 us
  Pallas kernels  84.8 us (90%)
  local copies, waits for them, and re-layouts  4.91 us (5%)
  other arithmetic  2.93 us (3%)
    pallas_call x1, Pallas kernels, kernel_body(): pl.pallas_call(functools.partial(step_kernel, (labs, dps, own, beam, pick...  84.8 us
    unnamed x2, local copies, waits for them, and re-layouts  4.91 us

profile of v4, /device:TPU:0, one launch (start us, length us, event | category | flops | bytes accessed | tf_op | source)
XLA Modules:
  0.0 93.3 jit_solution(8007990498029922022)
XLA Ops:
  0.6 0.8 select_reduce_fusion.1
  1.4 0.7 add_select_fusion.1
  2.2 0.7 copy_bitcast_fusion
  3.0 0.6 fusion.ids_ref
  3.6 84.8 %shard_map.68 = (bf16[2,128,1024]{2,1,0:T(8,128)(2,1)}, f32[2,1024,256]{2,1,0:T(8,128)}) custom-call(bf16[2,128,1024]{2,1,0:T(8,128)(2,1)} %bitcast.10, f32[2,24,128]{2,1,0:T(8,128)} %fusion.ids_ref, bf16[4,1024,256]{2,1,0:T(8,128)(2,1)} %panel_ref.1), custom_call_target="tpu_custom_call" | custom-call | tf_op jit(solution)/shard_map/pallas_call | solution.py:348
  88.4 1.9 %copy.18 = bf16[256,1024]{1,0:T(8,128)(2,1)} copy(bf16[256,1024]{1,0:T(8,128)(2,1)} %bitcast.11) | data formatting | bytes 1048576
  90.3 3.0 %copy.19 = f32[2,1024,256]{2,1,0:T(8,128)} copy(f32[2,1024,256]{2,1,0:T(8,128)} %get-tuple-element.9) | data formatting | bytes 4194304
  (1 shorter events, 0.0 us)
